TPU v7x, 256 devices: a whole 4x4x8 slice. The times are simulated.
256 devices in a mesh: tx: 8 (over x, y_hi), ty: 32 (over y_lo, z, core).
Axes of the slice: x: 4, y: 4 (y_hi: 2, y_lo: 2; y = y_hi * 2 + y_lo), z: 8, core: 2. Of those that a mesh axis runs over, the one named last changes fastest.
Arguments:
- features: bfloat16 [1536, 32, 512], P(('tx', 'ty')), may hold values from -6 to 6
- occupancy: int32 [1536, 512], P(('tx', 'ty')), may hold values from 0 to 1, as said below
- neighbours: int32 [1536, 6], P(('tx', 'ty')), may hold values from -1 to 1535, as said below
- w_first: bfloat16 [32, 864], replicated, may hold values from -0.21875 to 0.21875
- w_second: bfloat16 [32, 864], replicated, may hold values from -0.21875 to 0.21875
- cotangent: bfloat16 [1536, 32, 512], P(('tx', 'ty')), may hold values from -6 to 6
Outputs:
- result: bfloat16 [1536, 32, 512], P(('tx', 'ty'))
- grad_features: bfloat16 [1536, 32, 512], P(('tx', 'ty'))
- grad_first: float32 [32, 864], replicated
- grad_second: float32 [32, 864], replicated
Inputs may be any that keep to these rules, and one draw needn't show every extreme that they name: Bricks lie on a lattice of 16 x 96 x 1 positions; the tile of device (tx, ty) (brick rows of index tx * 32 + ty) holds positions with x in [tx * 2, (tx+1) * 2) and y in [ty * 3, (ty+1) * 3), one slot each in a drawn order. An id is device * 6 + slot. A neighbour across faces 0 and 1 lies on the same device or on the device one step lower or higher along tx with the same ty; across faces 2 and 3 on the same device or one step along ty; across faces 4 and 5 on the same device. If neighbours[s, f] = t then neighbours[t, f^1] = s. Inactive bricks have all entries -1 and no occupied voxels. `occupancy`: only active bricks have occupied voxels.
All inputs are finite; a program needn't handle non-finite values.
Results may differ from a plain program's by a relative error of at most 0.03.
The roundings to bfloat16 on the way count: a program that leaves them out, or rounds other values in their place, can miss the bound.
Values may be sent and summed in bfloat16 or wider, within the bound.
No kernel may reach another device: no remote copies, remote signals or barrier semaphores. Data moves between devices by JAX's collectives and lax.ppermute only.
A program may use at most 128 MiB of HBM per device.

v0:
```python
import math
import jax
import jax.numpy as jnp
from jax import lax
from jax.sharding import PartitionSpec as P

EDGE = 8


def passed_along(value, axis, steps):
    count = lax.axis_size(axis)
    first, last = (max(0, -steps), min(count, count - steps))
    return lax.ppermute(value, axis, [(source, source + steps) for source in range(first, last)])


def face_planes(field):
    count, chans = (field.shape[0], field.shape[1])
    cube = field.reshape(count, chans, EDGE, EDGE, EDGE)
    faces = [
        cube[:, :, 0],
        cube[:, :, -1],
        cube[:, :, :, 0],
        cube[:, :, :, -1],
        cube[:, :, :, :, 0],
        cube[:, :, :, :, -1],
    ]
    return [face.reshape(count, chans, EDGE * EDGE) for face in faces]


def forward_remote(items):
    return [
        passed_along(items[1], "tx", 1),
        passed_along(items[0], "tx", -1),
        passed_along(items[3], "ty", 1),
        passed_along(items[2], "ty", -1),
    ]


def backward_remote(items):
    return [
        passed_along(items[1].astype(jnp.bfloat16), "tx", 1).astype(jnp.float32),
        passed_along(items[0].astype(jnp.bfloat16), "tx", -1).astype(jnp.float32),
        passed_along(items[3].astype(jnp.bfloat16), "ty", 1).astype(jnp.float32),
        passed_along(items[2].astype(jnp.bfloat16), "ty", -1).astype(jnp.float32),
    ]


def collect_every(items, neighbours, myself, remote_fn):
    slots = items[0].shape[0]
    result = []
    remote = remote_fn(items)
    for face in range(6):
        ident = neighbours[:, face]
        valid = (ident >= 0).astype(items[0].dtype)
        safe = jnp.maximum(ident, 0)
        local = safe % slots
        if face < 4:
            owner = safe // slots
            source = jnp.concatenate([items[face ^ 1], remote[face]], axis=0)
            pick = local + slots * (owner != myself).astype(jnp.int32)
        else:
            source = items[face ^ 1]
            pick = local
        result.append(jnp.take(source, pick, axis=0) * valid[:, None, None])
    return result


def collect(items, neighbours, myself):
    return collect_every(items, neighbours, myself, forward_remote)


def padded(field, halos):
    count, chans = (field.shape[0], field.shape[1])
    cube = field.reshape(count, chans, EDGE, EDGE, EDGE)
    cells = jnp.pad(cube, ((0, 0), (0, 0), (1, 1), (1, 1), (1, 1)))
    sheet = [h.reshape(count, chans, EDGE, EDGE) for h in halos]
    cells = cells.at[:, :, 0, 1:-1, 1:-1].set(sheet[0])
    cells = cells.at[:, :, -1, 1:-1, 1:-1].set(sheet[1])
    cells = cells.at[:, :, 1:-1, 0, 1:-1].set(sheet[2])
    cells = cells.at[:, :, 1:-1, -1, 1:-1].set(sheet[3])
    cells = cells.at[:, :, 1:-1, 1:-1, 0].set(sheet[4])
    cells = cells.at[:, :, 1:-1, 1:-1, -1].set(sheet[5])
    return cells


def columns(block):
    count, chans = (block.shape[0], block.shape[1])
    pieces = []
    for first in range(3):
        for second in range(3):
            for third in range(3):
                piece = block[
                    :, :, first : first + EDGE, second : second + EDGE, third : third + EDGE
                ]
                pieces.append(piece.reshape(count, chans, EDGE * EDGE * EDGE))
    return jnp.concatenate(pieces, axis=1)


def conv_blocks(cells, weight, group):
    count = cells.shape[0]
    blocks = cells.reshape((count // group, group) + cells.shape[1:])

    def conv_one_block(block):
        return jnp.einsum("ok,gkv->gov", weight, columns(block), preferred_element_type=jnp.float32)

    out = lax.map(conv_one_block, blocks)
    return out.reshape(count, weight.shape[0], -1)


def weight_grad(cells, grad, group):
    count = cells.shape[0]
    blocks = cells.reshape((count // group, group) + cells.shape[1:])
    grads = grad.reshape((count // group, group) + grad.shape[1:])

    def weight_one_block(pair):
        return jnp.einsum(
            "gov,gkv->ok", pair[1], columns(pair[0]), preferred_element_type=jnp.float32
        )

    return jnp.sum(lax.map(weight_one_block, (blocks, grads)), axis=0)


def spread_taps(spread):
    count = spread.shape[0]
    chans = spread.shape[1] // 27
    cells = jnp.zeros((count, chans, EDGE + 2, EDGE + 2, EDGE + 2), jnp.float32)
    tap = 0
    for first in range(3):
        for second in range(3):
            for third in range(3):
                piece = spread[:, tap * chans : (tap + 1) * chans].reshape(
                    count, chans, EDGE, EDGE, EDGE
                )
                cells = cells.at[
                    :, :, first : first + EDGE, second : second + EDGE, third : third + EDGE
                ].add(piece)
                tap = tap + 1
    return cells


def transpose_returned(grad, weight, group, neighbours, myself):
    count, chans = (grad.shape[0], grad.shape[1])
    grads = grad.reshape((count // group, group) + grad.shape[1:])

    def transpose_one_block(block):
        spread = jnp.einsum("ok,gov->gkv", weight, block, preferred_element_type=jnp.float32)
        return spread_taps(spread)

    cells = lax.map(transpose_one_block, grads).reshape(count, chans, EDGE + 2, EDGE + 2, EDGE + 2)
    inner = cells[:, :, 1:-1, 1:-1, 1:-1]
    layers = [
        cells[:, :, 0, 1:-1, 1:-1],
        cells[:, :, -1, 1:-1, 1:-1],
        cells[:, :, 1:-1, 0, 1:-1],
        cells[:, :, 1:-1, -1, 1:-1],
        cells[:, :, 1:-1, 1:-1, 0],
        cells[:, :, 1:-1, 1:-1, -1],
    ]
    layers = [layer.reshape(count, chans, EDGE * EDGE) for layer in layers]
    landed = collect_every(layers, neighbours, myself, backward_remote)
    sheet = [piece.reshape(count, chans, EDGE, EDGE) for piece in landed]
    inner = inner.at[:, :, 0].add(sheet[0])
    inner = inner.at[:, :, -1].add(sheet[1])
    inner = inner.at[:, :, :, 0].add(sheet[2])
    inner = inner.at[:, :, :, -1].add(sheet[3])
    inner = inner.at[:, :, :, :, 0].add(sheet[4])
    inner = inner.at[:, :, :, :, -1].add(sheet[5])
    return inner.reshape(count, chans, EDGE * EDGE * EDGE)


def body(features, occupancy, neighbours, w_first, w_second, cotangent):
    slots = features.shape[0]
    group = 2
    myself = lax.axis_index("tx") * lax.axis_size("ty") + lax.axis_index("ty")
    mask = occupancy.astype(jnp.float32)[:, None, :]
    x_zero = (features.astype(jnp.float32) * mask).astype(jnp.bfloat16)
    pad_x = padded(x_zero, collect(face_planes(x_zero), neighbours, myself))
    pre_one = conv_blocks(pad_x, w_first, group)
    hidden = (jnp.maximum(pre_one, 0.0) * mask).astype(jnp.bfloat16)
    pad_h = padded(hidden, collect(face_planes(hidden), neighbours, myself))
    pre_two = conv_blocks(pad_h, w_second, group) + x_zero.astype(jnp.float32)
    result = (jnp.maximum(pre_two, 0.0) * mask).astype(jnp.bfloat16)
    grad_two = jnp.where(pre_two > 0.0, cotangent.astype(jnp.float32) * mask, 0.0).astype(
        jnp.bfloat16
    )
    term_second = weight_grad(pad_h, grad_two, group)
    dhidden = transpose_returned(grad_two, w_second, group, neighbours, myself)
    grad_one = jnp.where(pre_one > 0.0, dhidden * mask, 0.0).astype(jnp.bfloat16)
    term_first = weight_grad(pad_x, grad_one, group)
    dinput = transpose_returned(grad_one, w_first, group, neighbours, myself)
    grad_features = ((dinput + grad_two.astype(jnp.float32)) * mask).astype(jnp.bfloat16)
    total_first, total_second = lax.psum((term_first, term_second), ("tx", "ty"))
    scale = 1.0 / math.sqrt(slots * lax.axis_size("tx") * lax.axis_size("ty") * EDGE * EDGE * EDGE)
    return (result, grad_features, total_first * scale, total_second * scale)


def solution(mesh):
    return jax.shard_map(
        body,
        mesh=mesh,
        in_specs=(
            P(("tx", "ty"), None, None),
            P(("tx", "ty"), None),
            P(("tx", "ty"), None),
            P(),
            P(),
            P(("tx", "ty"), None, None),
        ),
        out_specs=(P(("tx", "ty"), None, None), P(("tx", "ty"), None, None), P(), P()),
        check_vma=False,
    )
```

profile of v0, /device:TPU:2, one launch (start us, length us, event | category | flops | bytes accessed | tf_op | source)
XLA Modules:
  0.0 1238.3 jit_solution(17558030082121253444)
XLA Ops:
  9.8 5.1 collective-permute-start
  39.5 6.1 scatter.46
  45.6 6.0 scatter.49
  52.4 70.2 %while.144 = (s32[]{:T(128)}, f32[3,2,32,512]{3,2,1,0:T(8,128)}, bf16[3,2,32,10,10,10]{2,5,4,3,1,0:T(8,128)(2,1)}, bf16[32,864]{1,0:T(8,128)(2,1)S(1)}, s32[]{:T(128)}) while((s32[]{:T(128)}, f32[3,2,32,512]{3,2,1,0:T(8,128)}, bf16[3,2,32,10,10,10]{2,5,4,3,1,0:T(8,128)(2,1)}, bf16[32,864]{1,0:T(8,128)(2,1)S(1)}, s32[]{:T(128)}) %tuple.690), condition=%wide.region_1.4_spmd, body=%wide.region_0.3_spmd.sunk | while | flops 56623104 | bytes 14402281 | solution.py:106
  127.4 5.8 collective-permute-start.6
  133.2 4.2 collective-permute-start.5
  155.0 6.0 scatter.56
  161.0 6.0 scatter.59
  167.9 69.9 %while.145 = (s32[]{:T(128)}, f32[3,2,32,512]{3,2,1,0:T(8,128)}, bf16[3,2,32,10,10,10]{2,5,4,3,1,0:T(8,128)(2,1)}, bf16[32,864]{1,0:T(8,128)(2,1)S(1)}, s32[]{:T(128)}) while((s32[]{:T(128)}, f32[3,2,32,512]{3,2,1,0:T(8,128)}, bf16[3,2,32,10,10,10]{2,5,4,3,1,0:T(8,128)(2,1)}, bf16[32,864]{1,0:T(8,128)(2,1)S(1)}, s32[]{:T(128)}) %tuple.688), condition=%wide.region_3.6_spmd, body=%wide.region_2.5_spmd.sunk | while | flops 56623104 | bytes 14402281 | solution.py:106
  245.9 249.1 %while.146 = (s32[]{:T(128)}, f32[3,2,32,10,10,10]{2,5,4,1,0,3:T(8,128)}, bf16[3,2,32,512]{3,2,1,0:T(8,128)(2,1)}, bf16[32,864]{1,0:T(8,128)(2,1)S(1)}, s32[]{:T(128)}, /*index=5*/f32[]{:T(128)}, s32[]{:T(128)}, s32[]{:T(128)}) while((s32[]{:T(128)}, f32[3,2,32,10,10,10]{2,5,4,1,0,3:T(8,128)}, bf16[3,2,32,512]{3,2,1,0:T(8,128)(2,1)}, ...), condition=%wide.region_5.8_spmd, body=%wide.region_4.7_spmd.sunk | while | flops 57475072 | bytes 60730716 | solution.py:149
  274.0 4.8 scatter-add.437
  353.0 4.8 scatter-add.437
  432.0 4.8 scatter-add.437
  505.0 4.3 collective-permute-start.10
  509.3 5.1 collective-permute-start.9
  520.3 73.0 %while.149 = (s32[]{:T(128)}, f32[3,32,864]{2,1,0:T(8,128)}, bf16[3,2,32,512]{3,2,1,0:T(8,128)(2,1)}, bf16[3,2,32,10,10,10]{2,5,4,3,1,0:T(8,128)(2,1)}, s32[]{:T(128)}) while((s32[]{:T(128)}, f32[3,32,864]{2,1,0:T(8,128)}, bf16[3,2,32,512]{3,2,1,0:T(8,128)(2,1)}, bf16[3,2,32,10,10,10]{2,5,4,3,1,0:T(8,128)(2,1)}, s32[]{:T(128)}) %tuple.682), condition=%wide.region_13.18_spmd, body=%wide.region_12.17_spmd.sunk | while | flops 56623104 | bytes 14396649 | solution.py:120
  612.1 4.0 scatter-add.253
  624.8 237.2 %while.147 = (s32[]{:T(128)}, f32[3,2,32,10,10,10]{2,5,4,1,0,3:T(8,128)}, bf16[3,2,32,512]{3,2,1,0:T(8,128)(2,1)}, bf16[32,864]{1,0:T(8,128)(2,1)S(1)}, s32[]{:T(128)}, /*index=5*/f32[]{:T(128)}, s32[]{:T(128)}, s32[]{:T(128)}) while((s32[]{:T(128)}, f32[3,2,32,10,10,10]{2,5,4,1,0,3:T(8,128)}, bf16[3,2,32,512]{3,2,1,0:T(8,128)(2,1)}, ...), condition=%wide.region_7.12_spmd, body=%wide.region_6.11_spmd.sunk | while | flops 57475072 | bytes 60730716 | solution.py:149
  641.3 4.6 scatter-add.465
  720.3 4.6 scatter-add.465
  799.2 4.6 scatter-add.465
  871.6 73.1 %while.148 = (s32[]{:T(128)}, f32[3,32,864]{2,1,0:T(8,128)}, bf16[3,2,32,512]{3,2,1,0:T(8,128)(2,1)}, bf16[3,2,32,10,10,10]{2,5,4,3,1,0:T(8,128)(2,1)}, s32[]{:T(128)}) while((s32[]{:T(128)}, f32[3,32,864]{2,1,0:T(8,128)}, bf16[3,2,32,512]{3,2,1,0:T(8,128)(2,1)}, bf16[3,2,32,10,10,10]{2,5,4,3,1,0:T(8,128)(2,1)}, s32[]{:T(128)}) %tuple.679), condition=%wide.region_9.14_spmd, body=%wide.region_8.13_spmd.sunk | while | flops 56623104 | bytes 14396649 | solution.py:120
  952.3 6.0 collective-permute-start.13
  986.0 242.0 %all-reduce.7.cloned.1.call-done = (f32[32,864]{1,0:T(8,128)}, f32[32,864]{1,0:T(8,128)}) async-done(((f32[32,864]{1,0:T(8,128)}, f32[32,864]{1,0:T(8,128)}), (f32[32,864]{1,0:T(8,128)}, f32[32,864]{1,0:T(8,128)})) %all-reduce.7.cloned.1.call-update) | async-done | bytes 221200 | tf_op jit(solution)/shard_map/psum | solution.py:192
  (1714 shorter events, 871.7 us)
Async XLA Ops:
  7.2 1220.8 %all-reduce.7.cloned.1.call-start = ((), (), s32[]{:S(2)}) async-start(), calls=%async_computation | async-start | bytes 458752 | tf_op jit(solution)/shard_map/psum | solution.py:192
  7.9 231.4 %copy-start.56 = (f32[6,512]{1,0:T(8,128)}, f32[6,512]{1,0:T(8,128)S(1)}, u32[]{:S(2)}) copy-start(f32[6,512]{1,0:T(8,128)S(1)} %convert_element_type.223) | copy-start | bytes 36868
  9.8 19.9 %collective-permute-start = (bf16[6,32,64]{1,2,0:T(8,128)(2,1)S(1)}, bf16[6,32,64]{1,2,0:T(8,128)(2,1)S(1)}, u32[]{:S(2)}, u32[]{:S(2)}) collective-permute-start(bf16[6,32,64]{1,2,0:T(8,128)(2,1)S(1)} %get-tuple-element.1689), channel_id=1, source_target_pairs={{0,32},{32,64},{64,96},{96,128},{128,160},{160,192},{192,224},{1,3... | collective-permute-start | bytes 73736 | tf_op jit(solution)/shard_map/ppermute | solution.py:13
  14.9 14.8 %collective-permute-start.1 = (bf16[6,32,64]{1,2,0:T(8,128)(2,1)S(1)}, bf16[6,32,64]{1,2,0:T(8,128)(2,1)S(1)}, u32[]{:S(2)}, u32[]{:S(2)}) collective-permute-start(bf16[6,32,64]{1,2,0:T(8,128)(2,1)S(1)} %get-tuple-element.1688), channel_id=1, source_target_pairs={{32,0},{64,32},{96,64},{128,96},{160,128},{192,160},{224,192},{33,... | collective-permute-start | bytes 73736 | tf_op jit(solution)/shard_map/ppermute | solution.py:13
  18.1 12.8 %collective-permute-start.2 = (bf16[6,32,64]{1,2,0:T(8,128)(2,1)S(1)}, bf16[6,32,64]{1,2,0:T(8,128)(2,1)S(1)}, u32[]{:S(2)}, u32[]{:S(2)}) collective-permute-start(bf16[6,32,64]{1,2,0:T(8,128)(2,1)S(1)} %get-tuple-element.1687), channel_id=1, source_target_pairs={{0,1},{1,2},{2,3},{3,4},{4,5},{5,6},{6,7},{7,8},{8,9},{9,10},{10,1... | collective-permute-start | bytes 73736 | tf_op jit(solution)/shard_map/ppermute | solution.py:13
  19.4 17.7 %collective-permute-start.3 = (bf16[6,32,64]{1,2,0:T(8,128)(2,1)S(1)}, bf16[6,32,64]{1,2,0:T(8,128)(2,1)S(1)}, u32[]{:S(2)}, u32[]{:S(2)}) collective-permute-start(bf16[6,32,64]{1,2,0:T(8,128)(2,1)S(1)} %get-tuple-element.1686), channel_id=1, source_target_pairs={{1,0},{2,1},{3,2},{4,3},{5,4},{6,5},{7,6},{8,7},{9,8},{10,9},{11,1... | collective-permute-start | bytes 73736 | tf_op jit(solution)/shard_map/ppermute | solution.py:13
  22.4 125.6 %copy-start.61 = (pred[6]{0:T(512)(128)(4,1)}, pred[6]{0:T(512)(128)(4,1)S(1)}, u32[]{:S(2)}) copy-start(pred[6]{0:T(512)(128)(4,1)S(1)} %get-tuple-element.1490) | copy-start | bytes 22
  22.6 124.6 %copy-start.64 = (pred[6]{0:T(512)(128)(4,1)}, pred[6]{0:T(512)(128)(4,1)S(1)}, u32[]{:S(2)}) copy-start(pred[6]{0:T(512)(128)(4,1)S(1)} %get-tuple-element.1488) | copy-start | bytes 22
  22.8 122.9 %copy-start.82 = (s32[1024]{0:T(1024)}, s32[1024]{0:T(1024)S(1)}, u32[]{:S(2)}) copy-start(s32[1024]{0:T(1024)S(1)} %pad_clamp_fusion.3) | copy-start | bytes 12292
  22.9 122.6 %copy-start.71 = (pred[6]{0:T(512)(128)(4,1)}, pred[6]{0:T(512)(128)(4,1)S(1)}, u32[]{:S(2)}) copy-start(pred[6]{0:T(512)(128)(4,1)S(1)} %get-tuple-element.1484) | copy-start | bytes 22
  22.9 122.0 %copy-start.83 = (s32[1024]{0:T(1024)}, s32[1024]{0:T(1024)S(1)}, u32[]{:S(2)}) copy-start(s32[1024]{0:T(1024)S(1)} %pad_clamp_fusion.2) | copy-start | bytes 12292
  23.0 119.4 %copy-start.74 = (pred[6]{0:T(512)(128)(4,1)}, pred[6]{0:T(512)(128)(4,1)S(1)}, u32[]{:S(2)}) copy-start(pred[6]{0:T(512)(128)(4,1)S(1)} %get-tuple-element.1480) | copy-start | bytes 22
  126.1 18.8 %collective-permute-start.7 = (bf16[6,32,64]{1,2,0:T(8,128)(2,1)S(1)}, bf16[6,32,64]{1,2,0:T(8,128)(2,1)S(1)}, u32[]{:S(2)}, u32[]{:S(2)}) collective-permute-start(bf16[6,32,64]{1,2,0:T(8,128)(2,1)S(1)} %get-tuple-element.1680), channel_id=1, source_target_pairs={{1,0},{2,1},{3,2},{4,3},{5,4},{6,5},{7,6},{8,7},{9,8},{10,9},{11,1... | collective-permute-start | bytes 73736 | tf_op jit(solution)/shard_map/ppermute | solution.py:13
  127.4 18.3 %collective-permute-start.6 = (bf16[6,32,64]{1,2,0:T(8,128)(2,1)S(1)}, bf16[6,32,64]{1,2,0:T(8,128)(2,1)S(1)}, u32[]{:S(2)}, u32[]{:S(2)}) collective-permute-start(bf16[6,32,64]{1,2,0:T(8,128)(2,1)S(1)} %get-tuple-element.1681), channel_id=1, source_target_pairs={{0,1},{1,2},{2,3},{3,4},{4,5},{5,6},{6,7},{7,8},{8,9},{9,10},{10,1... | collective-permute-start | bytes 73736 | tf_op jit(solution)/shard_map/ppermute | solution.py:13
  133.2 13.2 %collective-permute-start.5 = (bf16[6,32,64]{1,2,0:T(8,128)(2,1)S(1)}, bf16[6,32,64]{1,2,0:T(8,128)(2,1)S(1)}, u32[]{:S(2)}, u32[]{:S(2)}) collective-permute-start(bf16[6,32,64]{1,2,0:T(8,128)(2,1)S(1)} %get-tuple-element.1682), channel_id=1, source_target_pairs={{32,0},{64,32},{96,64},{128,96},{160,128},{192,160},{224,192},{33,... | collective-permute-start | bytes 73736 | tf_op jit(solution)/shard_map/ppermute | solution.py:13
  137.4 9.9 collective-permute-start.4
  503.1 98.1 %collective-permute-start.11 = (bf16[6,32,64]{1,2,0:T(8,128)(2,1)}, bf16[6,32,64]{1,2,0:T(8,128)(2,1)}, u32[]{:S(2)}, u32[]{:S(2)}) collective-permute-start(bf16[6,32,64]{1,2,0:T(8,128)(2,1)} %bitcast.399), channel_id=1, source_target_pairs={{1,0},{2,1},{3,2},{4,3},{5,4},{6,5},{7,6},{8,7},{9,8},{10,9},{11,1... | collective-permute-start | bytes 73736 | tf_op jit(solution)/shard_map/ppermute | solution.py:13
  505.0 97.1 %collective-permute-start.10 = (bf16[6,32,64]{1,2,0:T(8,128)(2,1)}, bf16[6,32,64]{1,2,0:T(8,128)(2,1)}, u32[]{:S(2)}, u32[]{:S(2)}) collective-permute-start(bf16[6,32,64]{1,2,0:T(8,128)(2,1)} %bitcast.398), channel_id=1, source_target_pairs={{0,1},{1,2},{2,3},{3,4},{4,5},{5,6},{6,7},{7,8},{8,9},{9,10},{10,1... | collective-permute-start | bytes 73736 | tf_op jit(solution)/shard_map/ppermute | solution.py:13
  509.3 94.5 %collective-permute-start.9 = (bf16[6,32,64]{1,2,0:T(8,128)(2,1)}, bf16[6,32,64]{1,2,0:T(8,128)(2,1)}, u32[]{:S(2)}, u32[]{:S(2)}) collective-permute-start(bf16[6,32,64]{1,2,0:T(8,128)(2,1)} %get-tuple-element.1674), channel_id=1, source_target_pairs={{32,0},{64,32},{96,64},{128,96},{160,128},{192,160},{224,192},{33,... | collective-permute-start | bytes 73736 | tf_op jit(solution)/shard_map/ppermute | solution.py:13
  514.4 94.2 %collective-permute-start.8 = (bf16[6,32,64]{1,2,0:T(8,128)(2,1)}, bf16[6,32,64]{1,2,0:T(8,128)(2,1)}, u32[]{:S(2)}, u32[]{:S(2)}) collective-permute-start(bf16[6,32,64]{1,2,0:T(8,128)(2,1)} %get-tuple-element.1675), channel_id=1, source_target_pairs={{0,32},{32,64},{64,96},{96,128},{128,160},{160,192},{192,224},{1,3... | collective-permute-start | bytes 73736 | tf_op jit(solution)/shard_map/ppermute | solution.py:13
  945.7 21.0 %collective-permute-start.15 = (bf16[6,32,64]{1,2,0:T(8,128)(2,1)S(1)}, bf16[6,32,64]{1,2,0:T(8,128)(2,1)S(1)}, u32[]{:S(2)}, u32[]{:S(2)}) collective-permute-start(bf16[6,32,64]{1,2,0:T(8,128)(2,1)S(1)} %bitcast.985), channel_id=1, source_target_pairs={{1,0},{2,1},{3,2},{4,3},{5,4},{6,5},{7,6},{8,7},{9,8},{10,9},{11,1... | collective-permute-start | bytes 73736 | tf_op jit(solution)/shard_map/ppermute | solution.py:13
  948.6 18.2 %collective-permute-start.14 = (bf16[6,32,64]{1,2,0:T(8,128)(2,1)}, bf16[6,32,64]{1,2,0:T(8,128)(2,1)}, u32[]{:S(2)}, u32[]{:S(2)}) collective-permute-start(bf16[6,32,64]{1,2,0:T(8,128)(2,1)} %bitcast.400), channel_id=1, source_target_pairs={{0,1},{1,2},{2,3},{3,4},{4,5},{5,6},{6,7},{7,8},{8,9},{9,10},{10,1... | collective-permute-start | bytes 73736 | tf_op jit(solution)/shard_map/ppermute | solution.py:13
  952.3 16.2 %collective-permute-start.13 = (bf16[6,32,64]{1,2,0:T(8,128)(2,1)}, bf16[6,32,64]{1,2,0:T(8,128)(2,1)}, u32[]{:S(2)}, u32[]{:S(2)}) collective-permute-start(bf16[6,32,64]{1,2,0:T(8,128)(2,1)} %get-tuple-element.1666), channel_id=1, source_target_pairs={{32,0},{64,32},{96,64},{128,96},{160,128},{192,160},{224,192},{33,... | collective-permute-start | bytes 73736 | tf_op jit(solution)/shard_map/ppermute | solution.py:13
  958.3 14.3 %collective-permute-start.12 = (bf16[6,32,64]{1,2,0:T(8,128)(2,1)}, bf16[6,32,64]{1,2,0:T(8,128)(2,1)}, u32[]{:S(2)}, u32[]{:S(2)}) collective-permute-start(bf16[6,32,64]{1,2,0:T(8,128)(2,1)} %get-tuple-element.1667), channel_id=1, source_target_pairs={{0,32},{32,64},{64,96},{96,128},{128,160},{160,192},{192,224},{1,3... | collective-permute-start | bytes 73736 | tf_op jit(solution)/shard_map/ppermute | solution.py:13
  (171 other events, 1510.7 us)
Sparse Core Ops, SparseCore 0:
  966.8 261.1 all-reduce.6
where the time goes:
time: 1260 us; the launch traced here: 1240 us
  local copies, waits for them, and re-layouts  823 us (65%)
  waiting for transfers between devices  242 us (19%)
  other arithmetic  55.3 us (4%)
  starting transfers between devices  51.5 us (4%)
  matrix products  28.2 us (2%)
  loops' own time  21.4 us (2%)
  between operations  16.4 us (1%)
    scatter-add x114, local copies, waits for them, and re-layouts, spread_taps(): cells = cells.at[:, :, first:first + EDGE, second:second + EDGE, third:th...  317 us
    psum x1, waiting for transfers between devices, body(): lax.psum((term_first, term_second), ('tx', 'ty'))  242 us
    reshape x324, local copies, waits for them, and re-layouts, columns(): pieces.append(piece.reshape(count, chans, EDGE * EDGE * EDGE))  198 us
    slice x174, local copies, waits for them, and re-layouts, spread_taps(): spread[:, tap * chans:(tap + 1) * chans]  93.9 us
    ppermute x16, starting transfers between devices, passed_along(): lax.ppermute(value, axis, [(source, source + steps) for source in range(f...  51.4 us
    slice x24, local copies, waits for them, and re-layouts, columns(): block[:, :, first:first + EDGE, second:second + EDGE, third:third + EDGE]  46.2 us
  transfers between devices with their start and end apart: 17, of which 1 were waited for; matrix products, arithmetic and copies ran while one was open for 11% of the time, Pallas kernels for 0%

commit v1 on v0

--- a/solution.py
+++ b/solution.py
@@ -189,7 +189,7 @@
     term_first = weight_grad(pad_x, grad_one, group)
     dinput = transpose_returned(grad_one, w_first, group, neighbours, myself)
     grad_features = ((dinput + grad_two.astype(jnp.float32)) * mask).astype(jnp.bfloat16)
-    total_first, total_second = lax.psum((term_first, term_second), ("tx", "ty"))
+    total_first, total_second = lax.psum(lax.psum((term_first, term_second), "tx"), "ty")
     scale = 1.0 / math.sqrt(slots * lax.axis_size("tx") * lax.axis_size("ty") * EDGE * EDGE * EDGE)
     return (result, grad_features, total_first * scale, total_second * scale)
 

time: 1260 us -> 1310 us (1.040)
  waiting for transfers between devices: 242 us -> 295 us
    psum x1 -> x2, waiting for transfers between devices: 242 us -> 295 us  [the longest x1 219 us: body(): lax.psum(lax.psum((term_first, term_second), 'tx'), 'ty')]
  transfers between devices with their start and end apart: 17 -> 18, of which waited for: 1 -> 2; matrix products, arithmetic and copies ran while one was open for 11% -> 11% of each run, Pallas kernels for 0% -> 0%
where the time goes in v1:
time: 1310 us; the launch traced here: 1290 us
  local copies, waits for them, and re-layouts  824 us (63%)
  waiting for transfers between devices  295 us (23%)
  other arithmetic  56.4 us (4%)
  starting transfers between devices  51.5 us (4%)
  matrix products  28.1 us (2%)
  loops' own time  21.4 us (2%)
  between operations  16.4 us (1%)
    scatter-add x114, local copies, waits for them, and re-layouts, spread_taps(): cells = cells.at[:, :, first:first + EDGE, second:second + EDGE, third:th...  316 us
    psum x1, waiting for transfers between devices, body(): lax.psum(lax.psum((term_first, term_second), 'tx'), 'ty')  219 us
    reshape x324, local copies, waits for them, and re-layouts, columns(): pieces.append(piece.reshape(count, chans, EDGE * EDGE * EDGE))  198 us
    slice x174, local copies, waits for them, and re-layouts, spread_taps(): spread[:, tap * chans:(tap + 1) * chans]  93.9 us
    psum x1, waiting for transfers between devices, body(): lax.psum((term_first, term_second), 'tx')  76.5 us
    ppermute x16, starting transfers between devices, passed_along(): lax.ppermute(value, axis, [(source, source + steps) for source in range(f...  51.4 us
    slice x24, local copies, waits for them, and re-layouts, columns(): block[:, :, first:first + EDGE, second:second + EDGE, third:third + EDGE]  46.3 us
  transfers between devices with their start and end apart: 18, of which 2 were waited for; matrix products, arithmetic and copies ran while one was open for 11% of the time, Pallas kernels for 0%

profile of v1, /device:TPU:2, one launch (start us, length us, event | category | flops | bytes accessed | tf_op | source)
XLA Modules:
  0.0 1293.5 jit_solution(12126922537417061663)
XLA Ops:
  9.8 5.1 collective-permute-start
  39.4 6.1 scatter.46
  45.4 6.1 scatter.49
  52.3 70.2 %while.144 = (s32[]{:T(128)}, f32[3,2,32,512]{3,2,1,0:T(8,128)}, bf16[3,2,32,10,10,10]{2,5,4,3,1,0:T(8,128)(2,1)}, bf16[32,864]{1,0:T(8,128)(2,1)S(1)}, s32[]{:T(128)}) while((s32[]{:T(128)}, f32[3,2,32,512]{3,2,1,0:T(8,128)}, bf16[3,2,32,10,10,10]{2,5,4,3,1,0:T(8,128)(2,1)}, bf16[32,864]{1,0:T(8,128)(2,1)S(1)}, s32[]{:T(128)}) %tuple.693), condition=%wide.region_1.4_spmd, body=%wide.region_0.3_spmd.sunk | while | flops 56623104 | bytes 14402281 | solution.py:106
  127.3 5.8 collective-permute-start.6
  133.1 4.2 collective-permute-start.5
  154.9 6.0 scatter.56
  160.9 6.0 scatter.59
  167.8 69.9 %while.145 = (s32[]{:T(128)}, f32[3,2,32,512]{3,2,1,0:T(8,128)}, bf16[3,2,32,10,10,10]{2,5,4,3,1,0:T(8,128)(2,1)}, bf16[32,864]{1,0:T(8,128)(2,1)S(1)}, s32[]{:T(128)}) while((s32[]{:T(128)}, f32[3,2,32,512]{3,2,1,0:T(8,128)}, bf16[3,2,32,10,10,10]{2,5,4,3,1,0:T(8,128)(2,1)}, bf16[32,864]{1,0:T(8,128)(2,1)S(1)}, s32[]{:T(128)}) %tuple.691), condition=%wide.region_3.6_spmd, body=%wide.region_2.5_spmd.sunk | while | flops 56623104 | bytes 14402281 | solution.py:106
  245.7 249.0 %while.146 = (s32[]{:T(128)}, f32[3,2,32,10,10,10]{2,5,4,1,0,3:T(8,128)}, bf16[3,2,32,512]{3,2,1,0:T(8,128)(2,1)}, bf16[32,864]{1,0:T(8,128)(2,1)S(1)}, s32[]{:T(128)}, /*index=5*/f32[]{:T(128)}, s32[]{:T(128)}, s32[]{:T(128)}) while((s32[]{:T(128)}, f32[3,2,32,10,10,10]{2,5,4,1,0,3:T(8,128)}, bf16[3,2,32,512]{3,2,1,0:T(8,128)(2,1)}, ...), condition=%wide.region_5.8_spmd, body=%wide.region_4.7_spmd.sunk | while | flops 57475072 | bytes 60730716 | solution.py:149
  273.8 4.8 scatter-add.437
  352.8 4.8 scatter-add.437
  431.8 4.8 scatter-add.437
  504.8 4.3 collective-permute-start.10
  509.1 5.1 collective-permute-start.9
  520.0 73.0 %while.149 = (s32[]{:T(128)}, f32[3,32,864]{2,1,0:T(8,128)}, bf16[3,2,32,512]{3,2,1,0:T(8,128)(2,1)}, bf16[3,2,32,10,10,10]{2,5,4,3,1,0:T(8,128)(2,1)}, s32[]{:T(128)}) while((s32[]{:T(128)}, f32[3,32,864]{2,1,0:T(8,128)}, bf16[3,2,32,512]{3,2,1,0:T(8,128)(2,1)}, bf16[3,2,32,10,10,10]{2,5,4,3,1,0:T(8,128)(2,1)}, s32[]{:T(128)}) %tuple.682), condition=%wide.region_14.19_spmd, body=%wide.region_13.18_spmd.sunk | while | flops 56623104 | bytes 14396649 | solution.py:120
  624.6 236.8 %while.147 = (s32[]{:T(128)}, f32[3,2,32,10,10,10]{2,5,4,1,0,3:T(8,128)}, bf16[3,2,32,512]{3,2,1,0:T(8,128)(2,1)}, bf16[32,864]{1,0:T(8,128)(2,1)S(1)}, s32[]{:T(128)}, /*index=5*/f32[]{:T(128)}, s32[]{:T(128)}, s32[]{:T(128)}) while((s32[]{:T(128)}, f32[3,2,32,10,10,10]{2,5,4,1,0,3:T(8,128)}, bf16[3,2,32,512]{3,2,1,0:T(8,128)(2,1)}, ...), condition=%wide.region_7.12_spmd, body=%wide.region_6.11_spmd.sunk | while | flops 57475072 | bytes 60730716 | solution.py:149
  641.0 4.6 scatter-add.465
  719.8 4.6 scatter-add.465
  798.5 4.6 scatter-add.465
  870.9 73.2 %while.148 = (s32[]{:T(128)}, f32[3,32,864]{2,1,0:T(8,128)}, bf16[3,2,32,512]{3,2,1,0:T(8,128)(2,1)}, bf16[3,2,32,10,10,10]{2,5,4,3,1,0:T(8,128)(2,1)}, s32[]{:T(128)}) while((s32[]{:T(128)}, f32[3,32,864]{2,1,0:T(8,128)}, bf16[3,2,32,512]{3,2,1,0:T(8,128)(2,1)}, bf16[3,2,32,10,10,10]{2,5,4,3,1,0:T(8,128)(2,1)}, s32[]{:T(128)}) %tuple.679), condition=%wide.region_9.14_spmd, body=%wide.region_8.13_spmd.sunk | while | flops 56623104 | bytes 14396649 | solution.py:120
  951.7 6.0 collective-permute-start.13
  985.0 76.5 %all-reduce.11.cloned.1.call-done = (f32[32,864]{1,0:T(8,128)}, f32[32,864]{1,0:T(8,128)}) async-done(((f32[32,864]{1,0:T(8,128)}, f32[32,864]{1,0:T(8,128)}), (f32[32,864]{1,0:T(8,128)}, f32[32,864]{1,0:T(8,128)})) %all-reduce.11.cloned.1.call-update) | async-done | bytes 221200 | tf_op jit(solution)/shard_map/psum | solution.py:192
  1064.3 218.9 %all-reduce.9.cloned.1.call-done = (f32[32,864]{1,0:T(8,128)}, f32[32,864]{1,0:T(8,128)}) async-done(((f32[32,864]{1,0:T(8,128)}, f32[32,864]{1,0:T(8,128)}), (f32[32,864]{1,0:T(8,128)}, f32[32,864]{1,0:T(8,128)})) %all-reduce.9.cloned.1.call-update) | async-done | bytes 221200 | tf_op jit(solution)/shard_map/psum | solution.py:192
  (1717 shorter events, 877.7 us)
Async XLA Ops:
  7.2 1054.3 %all-reduce.11.cloned.1.call-start = ((), (), s32[]{:S(2)}) async-start(), calls=%async_computation.1 | async-start | bytes 458752 | tf_op jit(solution)/shard_map/psum | solution.py:192
  7.9 231.3 %copy-start.56 = (f32[6,512]{1,0:T(8,128)}, f32[6,512]{1,0:T(8,128)S(1)}, u32[]{:S(2)}) copy-start(f32[6,512]{1,0:T(8,128)S(1)} %convert_element_type.223) | copy-start | bytes 36868
  9.8 19.8 %collective-permute-start = (bf16[6,32,64]{1,2,0:T(8,128)(2,1)S(1)}, bf16[6,32,64]{1,2,0:T(8,128)(2,1)S(1)}, u32[]{:S(2)}, u32[]{:S(2)}) collective-permute-start(bf16[6,32,64]{1,2,0:T(8,128)(2,1)S(1)} %get-tuple-element.1691), channel_id=1, source_target_pairs={{0,32},{32,64},{64,96},{96,128},{128,160},{160,192},{192,224},{1,3... | collective-permute-start | bytes 73736 | tf_op jit(solution)/shard_map/ppermute | solution.py:13
  14.9 14.8 %collective-permute-start.1 = (bf16[6,32,64]{1,2,0:T(8,128)(2,1)S(1)}, bf16[6,32,64]{1,2,0:T(8,128)(2,1)S(1)}, u32[]{:S(2)}, u32[]{:S(2)}) collective-permute-start(bf16[6,32,64]{1,2,0:T(8,128)(2,1)S(1)} %get-tuple-element.1690), channel_id=1, source_target_pairs={{32,0},{64,32},{96,64},{128,96},{160,128},{192,160},{224,192},{33,... | collective-permute-start | bytes 73736 | tf_op jit(solution)/shard_map/ppermute | solution.py:13
  18.1 12.8 collective-permute-start.2
  19.4 17.6 %collective-permute-start.3 = (bf16[6,32,64]{1,2,0:T(8,128)(2,1)S(1)}, bf16[6,32,64]{1,2,0:T(8,128)(2,1)S(1)}, u32[]{:S(2)}, u32[]{:S(2)}) collective-permute-start(bf16[6,32,64]{1,2,0:T(8,128)(2,1)S(1)} %get-tuple-element.1688), channel_id=1, source_target_pairs={{1,0},{2,1},{3,2},{4,3},{5,4},{6,5},{7,6},{8,7},{9,8},{10,9},{11,1... | collective-permute-start | bytes 73736 | tf_op jit(solution)/shard_map/ppermute | solution.py:13
  22.4 125.6 %copy-start.61 = (pred[6]{0:T(512)(128)(4,1)}, pred[6]{0:T(512)(128)(4,1)S(1)}, u32[]{:S(2)}) copy-start(pred[6]{0:T(512)(128)(4,1)S(1)} %get-tuple-element.1492) | copy-start | bytes 22
  22.5 124.5 %copy-start.64 = (pred[6]{0:T(512)(128)(4,1)}, pred[6]{0:T(512)(128)(4,1)S(1)}, u32[]{:S(2)}) copy-start(pred[6]{0:T(512)(128)(4,1)S(1)} %get-tuple-element.1490) | copy-start | bytes 22
  22.7 122.9 %copy-start.82 = (s32[1024]{0:T(1024)}, s32[1024]{0:T(1024)S(1)}, u32[]{:S(2)}) copy-start(s32[1024]{0:T(1024)S(1)} %pad_clamp_fusion.3) | copy-start | bytes 12292
  22.9 122.6 %copy-start.71 = (pred[6]{0:T(512)(128)(4,1)}, pred[6]{0:T(512)(128)(4,1)S(1)}, u32[]{:S(2)}) copy-start(pred[6]{0:T(512)(128)(4,1)S(1)} %get-tuple-element.1486) | copy-start | bytes 22
  22.9 122.0 %copy-start.83 = (s32[1024]{0:T(1024)}, s32[1024]{0:T(1024)S(1)}, u32[]{:S(2)}) copy-start(s32[1024]{0:T(1024)S(1)} %pad_clamp_fusion.2) | copy-start | bytes 12292
  126.0 18.8 %collective-permute-start.7 = (bf16[6,32,64]{1,2,0:T(8,128)(2,1)S(1)}, bf16[6,32,64]{1,2,0:T(8,128)(2,1)S(1)}, u32[]{:S(2)}, u32[]{:S(2)}) collective-permute-start(bf16[6,32,64]{1,2,0:T(8,128)(2,1)S(1)} %get-tuple-element.1682), channel_id=1, source_target_pairs={{1,0},{2,1},{3,2},{4,3},{5,4},{6,5},{7,6},{8,7},{9,8},{10,9},{11,1... | collective-permute-start | bytes 73736 | tf_op jit(solution)/shard_map/ppermute | solution.py:13
  127.3 18.3 %collective-permute-start.6 = (bf16[6,32,64]{1,2,0:T(8,128)(2,1)S(1)}, bf16[6,32,64]{1,2,0:T(8,128)(2,1)S(1)}, u32[]{:S(2)}, u32[]{:S(2)}) collective-permute-start(bf16[6,32,64]{1,2,0:T(8,128)(2,1)S(1)} %get-tuple-element.1683), channel_id=1, source_target_pairs={{0,1},{1,2},{2,3},{3,4},{4,5},{5,6},{6,7},{7,8},{8,9},{9,10},{10,1... | collective-permute-start | bytes 73736 | tf_op jit(solution)/shard_map/ppermute | solution.py:13
  133.1 13.2 %collective-permute-start.5 = (bf16[6,32,64]{1,2,0:T(8,128)(2,1)S(1)}, bf16[6,32,64]{1,2,0:T(8,128)(2,1)S(1)}, u32[]{:S(2)}, u32[]{:S(2)}) collective-permute-start(bf16[6,32,64]{1,2,0:T(8,128)(2,1)S(1)} %get-tuple-element.1684), channel_id=1, source_target_pairs={{32,0},{64,32},{96,64},{128,96},{160,128},{192,160},{224,192},{33,... | collective-permute-start | bytes 73736 | tf_op jit(solution)/shard_map/ppermute | solution.py:13
  137.3 9.9 collective-permute-start.4
  502.9 98.0 %collective-permute-start.11 = (bf16[6,32,64]{1,2,0:T(8,128)(2,1)}, bf16[6,32,64]{1,2,0:T(8,128)(2,1)}, u32[]{:S(2)}, u32[]{:S(2)}) collective-permute-start(bf16[6,32,64]{1,2,0:T(8,128)(2,1)} %bitcast.399), channel_id=1, source_target_pairs={{1,0},{2,1},{3,2},{4,3},{5,4},{6,5},{7,6},{8,7},{9,8},{10,9},{11,1... | collective-permute-start | bytes 73736 | tf_op jit(solution)/shard_map/ppermute | solution.py:13
  504.8 97.1 %collective-permute-start.10 = (bf16[6,32,64]{1,2,0:T(8,128)(2,1)}, bf16[6,32,64]{1,2,0:T(8,128)(2,1)}, u32[]{:S(2)}, u32[]{:S(2)}) collective-permute-start(bf16[6,32,64]{1,2,0:T(8,128)(2,1)} %bitcast.398), channel_id=1, source_target_pairs={{0,1},{1,2},{2,3},{3,4},{4,5},{5,6},{6,7},{7,8},{8,9},{9,10},{10,1... | collective-permute-start | bytes 73736 | tf_op jit(solution)/shard_map/ppermute | solution.py:13
  509.1 94.5 %collective-permute-start.9 = (bf16[6,32,64]{1,2,0:T(8,128)(2,1)}, bf16[6,32,64]{1,2,0:T(8,128)(2,1)}, u32[]{:S(2)}, u32[]{:S(2)}) collective-permute-start(bf16[6,32,64]{1,2,0:T(8,128)(2,1)} %get-tuple-element.1676), channel_id=1, source_target_pairs={{32,0},{64,32},{96,64},{128,96},{160,128},{192,160},{224,192},{33,... | collective-permute-start | bytes 73736 | tf_op jit(solution)/shard_map/ppermute | solution.py:13
  514.2 94.2 %collective-permute-start.8 = (bf16[6,32,64]{1,2,0:T(8,128)(2,1)}, bf16[6,32,64]{1,2,0:T(8,128)(2,1)}, u32[]{:S(2)}, u32[]{:S(2)}) collective-permute-start(bf16[6,32,64]{1,2,0:T(8,128)(2,1)} %get-tuple-element.1677), channel_id=1, source_target_pairs={{0,32},{32,64},{64,96},{96,128},{128,160},{160,192},{192,224},{1,3... | collective-permute-start | bytes 73736 | tf_op jit(solution)/shard_map/ppermute | solution.py:13
  945.1 21.0 %collective-permute-start.15 = (bf16[6,32,64]{1,2,0:T(8,128)(2,1)S(1)}, bf16[6,32,64]{1,2,0:T(8,128)(2,1)S(1)}, u32[]{:S(2)}, u32[]{:S(2)}) collective-permute-start(bf16[6,32,64]{1,2,0:T(8,128)(2,1)S(1)} %bitcast.985), channel_id=1, source_target_pairs={{1,0},{2,1},{3,2},{4,3},{5,4},{6,5},{7,6},{8,7},{9,8},{10,9},{11,1... | collective-permute-start | bytes 73736 | tf_op jit(solution)/shard_map/ppermute | solution.py:13
  948.0 18.2 %collective-permute-start.14 = (bf16[6,32,64]{1,2,0:T(8,128)(2,1)}, bf16[6,32,64]{1,2,0:T(8,128)(2,1)}, u32[]{:S(2)}, u32[]{:S(2)}) collective-permute-start(bf16[6,32,64]{1,2,0:T(8,128)(2,1)} %bitcast.400), channel_id=1, source_target_pairs={{0,1},{1,2},{2,3},{3,4},{4,5},{5,6},{6,7},{7,8},{8,9},{9,10},{10,1... | collective-permute-start | bytes 73736 | tf_op jit(solution)/shard_map/ppermute | solution.py:13
  951.7 16.3 %collective-permute-start.13 = (bf16[6,32,64]{1,2,0:T(8,128)(2,1)}, bf16[6,32,64]{1,2,0:T(8,128)(2,1)}, u32[]{:S(2)}, u32[]{:S(2)}) collective-permute-start(bf16[6,32,64]{1,2,0:T(8,128)(2,1)} %get-tuple-element.1668), channel_id=1, source_target_pairs={{32,0},{64,32},{96,64},{128,96},{160,128},{192,160},{224,192},{33,... | collective-permute-start | bytes 73736 | tf_op jit(solution)/shard_map/ppermute | solution.py:13
  957.6 14.4 %collective-permute-start.12 = (bf16[6,32,64]{1,2,0:T(8,128)(2,1)}, bf16[6,32,64]{1,2,0:T(8,128)(2,1)}, u32[]{:S(2)}, u32[]{:S(2)}) collective-permute-start(bf16[6,32,64]{1,2,0:T(8,128)(2,1)} %get-tuple-element.1669), channel_id=1, source_target_pairs={{0,32},{32,64},{64,96},{96,128},{128,160},{160,192},{192,224},{1,3... | collective-permute-start | bytes 73736 | tf_op jit(solution)/shard_map/ppermute | solution.py:13
  966.1 317.1 %all-reduce.9.cloned.1.call-start = ((), (), s32[]{:S(2)}) async-start(), calls=%async_computation | async-start | bytes 458752 | tf_op jit(solution)/shard_map/psum | solution.py:192
  (172 other events, 1776.9 us)
Sparse Core Ops, SparseCore 0:
  966.2 95.2 all-reduce.10
  1064.2 218.9 all-reduce.8
